TPU v7x, 1024 devices: a whole 4x4x32 slice. The times are simulated.
1024 devices in a mesh: ctx: 32 (over z), exp: 4 (over x), tp: 8 (over y, core).
Axes of the slice: x: 4, y: 4, z: 32, core: 2. Of those that a mesh axis runs over, the one named last changes fastest.
Arguments:
- queries: bfloat16 [65536, 4096], P(('ctx', 'exp'), 'tp'), may hold values from -6 to 6
- key_vectors: bfloat16 [65536, 4096], P(('ctx', 'exp'), 'tp'), may hold values from -6 to 6
- value_vectors: bfloat16 [65536, 4096], P(('ctx', 'exp'), 'tp'), may hold values from -6 to 6
- decay_rate: float32 [32], P('tp'), may hold values from 1e-07 to 0.05
- norm_gain: float32 [4096], P('tp'), may hold values from 0.5 to 1.5
Outputs:
- normed: bfloat16 [65536, 4096], P(('ctx', 'exp'), 'tp')
All inputs are finite; a program needn't handle non-finite values.
Results may differ from a plain program's by a relative error of at most 0.0052.
Values sent between devices are 32-bit elements; how exact they have to be, the bound alone decides.
A program may use at most 128 MiB of HBM per device.

v0:
```python
import jax
import jax.numpy as jnp
from jax import lax
from jax.sharding import PartitionSpec as P

HEADS = 32
HEAD_DIM = 128
BLK = 256


def carried_in(value, axis, join, neutral):
    count, mine = (lax.axis_size(axis), lax.axis_index(axis))
    pieces = jax.tree.map(lambda part: lax.all_gather(part, axis), value)
    subtotal = jax.tree.map(
        lambda part, zero: jnp.full_like(part, 0) + jnp.asarray(zero, part.dtype), value, neutral
    )

    def hop(position, subtotal):
        longer = join(subtotal, jax.tree.map(lambda part: part[position], pieces))
        return jax.tree.map(lambda new, old: jnp.where(position < mine, new, old), longer, subtotal)

    return lax.fori_loop(0, count - 1, hop, subtotal)


def chain_step(earlier, later):
    decay_early, state_early = earlier
    decay_late, state_late = later
    return (decay_early * decay_late, decay_late[:, None, None] * state_early + state_late)


def local(queries, key_vectors, value_vectors, decay_rate, norm_gain):
    row_count = queries.shape[0]
    head_local = decay_rate.shape[0]
    block_count = row_count // BLK
    query_blocks = queries.reshape(block_count, BLK, head_local, HEAD_DIM)
    key_blocks = key_vectors.reshape(block_count, BLK, head_local, HEAD_DIM)
    value_blocks = value_vectors.reshape(block_count, BLK, head_local, HEAD_DIM)
    offsets = jnp.arange(BLK, dtype=jnp.float32)
    spread = offsets[:, None] - offsets[None, :]
    causal = spread >= 0
    rates = decay_rate[:, None, None]
    weight = jnp.where(causal[None], jnp.exp(-rates * jnp.maximum(spread, 0.0)[None]), 0.0)
    inner_decay = jnp.exp(-decay_rate[None, :] * offsets[:, None])
    tail_decay = jnp.exp(-decay_rate[None, :] * (BLK - offsets)[:, None])
    block_decay = jnp.exp(-decay_rate * BLK)[:, None, None]
    local_parts = []
    block_terms = []
    own_state = jnp.zeros((head_local, HEAD_DIM, HEAD_DIM), jnp.float32)
    for block_index in range(block_count):
        query_block = query_blocks[block_index]
        key_block = key_blocks[block_index]
        value_block = value_blocks[block_index]
        scores = jnp.einsum(
            "thd,shd->hts", query_block, key_block, preferred_element_type=jnp.float32
        )
        mixing = (scores * weight).astype(jnp.bfloat16)
        local_parts.append(
            jnp.einsum("hts,she->the", mixing, value_block, preferred_element_type=jnp.float32)
        )
        scaled_keys = (key_block.astype(jnp.float32) * tail_decay[:, :, None]).astype(jnp.bfloat16)
        block_term = jnp.einsum(
            "shd,she->hde", scaled_keys, value_block, preferred_element_type=jnp.float32
        )
        block_terms.append(block_term)
        own_state = block_decay * own_state + block_term
    span_decay = jnp.exp(-decay_rate * row_count)
    identity = (jnp.ones_like(span_decay), jnp.zeros_like(own_state))
    unused, before = carried_in((span_decay, own_state), ("ctx", "exp"), chain_step, identity)
    carry_state = before
    pieces = []
    for block_index in range(block_count):
        state_low = carry_state.astype(jnp.bfloat16)
        carried = jnp.einsum(
            "thd,hde->the", query_blocks[block_index], state_low, preferred_element_type=jnp.float32
        )
        pieces.append(local_parts[block_index] + carried * inner_decay[:, :, None])
        carry_state = block_decay * carry_state + block_terms[block_index]
    attended = jnp.concatenate(pieces, axis=0).reshape(row_count, head_local * HEAD_DIM)
    row_squares = jnp.sum(attended * attended, axis=1)
    row_total = lax.psum(row_squares, "tp")
    mean_square = row_total / (HEADS * HEAD_DIM)
    normed = attended * lax.rsqrt(mean_square + 1e-06)[:, None] * norm_gain[None, :]
    return normed.astype(jnp.bfloat16)


def solution(mesh):
    return jax.shard_map(
        local,
        mesh=mesh,
        in_specs=(
            P(("ctx", "exp"), "tp"),
            P(("ctx", "exp"), "tp"),
            P(("ctx", "exp"), "tp"),
            P("tp"),
            P("tp"),
        ),
        out_specs=P(("ctx", "exp"), "tp"),
        check_vma=False,
    )
```

profile of v0, /device:TPU:1, one launch (start us, length us, event | category | flops | bytes accessed | tf_op | source)
XLA Modules:
  0.0 569.0 jit_solution(18412836093999201580)
XLA Ops:
  6.5 1.1 fusion.27
  7.8 1.1 fusion.28
  9.2 1.3 dynamic-slice
  13.2 241.2 %all-reduce = f32[512]{0:T(512)S(1)} all-reduce(f32[512]{0:T(512)S(1)} %get-tuple-element.137), channel_id=2, replica_groups=mesh['ctx'=32,'exp'=4,'tp'=8] {'ctx','exp'}, use_global_device_ids=true, to_apply=%add | all-reduce | flops 512 | bytes 4096
  254.5 1.1 fusion.26
  257.1 149.9 %all-gather.4.cloned.1.call-done = f32[512,128,128]{2,1,0:T(8,128)} async-done(((f32[4,128,128]{2,1,0:T(8,128)}), f32[512,128,128]{2,1,0:T(8,128)}) %all-gather.4.cloned.1.call-update) | async-done | bytes 33554448 | tf_op jit(solution)/shard_map/all_gather | solution.py:13
  407.0 138.9 %while.14 = (s32[]{:T(128)}, f32[4,128,128]{2,1,0:T(8,128)S(1)}, s32[]{:T(128)}, f32[128,4]{1,0:T(8,128)S(1)}, f32[128,4,128,128]{3,2,1,0:T(8,128)}, /*index=5*/s32[]{:T(128)}, s32[]{:T(128)}) while((s32[]{:T(128)}, f32[4,128,128]{2,1,0:T(8,128)S(1)}, s32[]{:T(128)}, f32[128,4]{1,0:T(8,128)S(1)}, f32[128,4,128,128]{3,2,1,0:T(8,128)}, ...), condition=%wide.region_1.2_spmd.clone, body=%wide.region_0.1_spmd.clone.sunk | while | flops 262148 | bytes 786585 | solution.py:22
  408.1 1.1 fusion.40
  409.2 1.1 fusion.40
  410.3 1.1 fusion.40
  413.6 1.1 fusion.40
  414.6 1.1 fusion.40
  415.7 1.1 fusion.40
  419.0 1.1 fusion.40
  420.1 1.1 fusion.40
  423.4 1.1 fusion.40
  424.5 1.1 fusion.40
  425.6 1.1 fusion.40
  428.9 1.1 fusion.40
  430.0 1.1 fusion.40
  431.0 1.1 fusion.40
  434.3 1.1 fusion.40
  435.4 1.1 fusion.40
  436.5 1.1 fusion.40
  439.8 1.1 fusion.40
  440.9 1.1 fusion.40
  444.2 1.1 fusion.40
  445.3 1.1 fusion.40
  446.4 1.1 fusion.40
  449.6 1.1 fusion.40
  450.7 1.1 fusion.40
  451.8 1.1 fusion.40
  455.1 1.1 fusion.40
  456.2 1.1 fusion.40
  457.3 1.1 fusion.40
  460.6 1.1 fusion.40
  461.7 1.1 fusion.40
  465.0 1.1 fusion.40
  466.0 1.1 fusion.40
  467.1 1.1 fusion.40
  470.4 1.1 fusion.40
  471.5 1.1 fusion.40
  472.6 1.1 fusion.40
  475.9 1.1 fusion.40
  477.0 1.1 fusion.40
  478.1 1.1 fusion.40
  481.4 1.1 fusion.40
  482.5 1.1 fusion.40
  485.7 1.1 fusion.40
  486.8 1.1 fusion.40
  487.9 1.1 fusion.40
  491.2 1.1 fusion.40
  492.3 1.1 fusion.40
  493.4 1.1 fusion.40
  496.7 1.1 fusion.40
  497.8 1.1 fusion.40
  498.9 1.1 fusion.40
  502.1 1.1 fusion.40
  503.2 1.1 fusion.40
  506.5 1.1 fusion.40
  507.6 1.1 fusion.40
  508.7 1.1 fusion.40
  512.0 1.1 fusion.40
  547.0 13.2 %psum.7 = f32[512]{0:T(512)S(1)} all-reduce(f32[512]{0:T(512)S(1)} %get-tuple-element.128), channel_id=1, replica_groups=mesh['ctx'=32,'exp'=4,'tp'=8] {'tp'}, use_global_device_ids=true, to_apply=%region_3.4 | all-reduce | flops 512 | bytes 4096 | tf_op jit(solution)/shard_map/psum | solution.py:80
  (225 shorter events, 83.1 us)
Async XLA Ops:
  6.5 400.4 %all-gather.4.cloned.1.call-start = ((), (), s32[]{:S(2)}) async-start(), calls=%async_computation | async-start | bytes 33816576 | tf_op jit(solution)/shard_map/all_gather | solution.py:13
Sparse Core Ops, SparseCore 0:
  13.3 393.6 all-gather.3
where the time goes:
time: 573 us; the launch traced here: 569 us
  blocking collectives  254 us (44%)
  waiting for transfers between devices  150 us (26%)
  other arithmetic  136 us (24%)
  between operations  14.2 us (2%)
  local copies, waits for them, and re-layouts  7.91 us (1%)
    unnamed x1, blocking collectives  241 us
    all_gather x1, waiting for transfers between devices, carried_in(): pieces = jax.tree.map(lambda part: lax.all_gather(part, axis), value)  150 us
    select_n x127, other arithmetic, hop(): jnp.where(position < mine, new, old)  134 us
    psum x1, blocking collectives, local(): row_total = lax.psum(row_squares, 'tp')  13.2 us
  transfers between devices with their start and end apart: 1, of which 1 were waited for; matrix products, arithmetic and copies ran while one was open for 0% of the time, Pallas kernels for 0%

commit v1 on v0

v1 whole, which is shorter than its diff:
```python
import functools

import jax
import jax.numpy as jnp
from jax import lax
from jax.experimental import pallas as pl
from jax.experimental.pallas import tpu as pltpu
from jax.sharding import PartitionSpec as P

HEADS = 32
HEAD_DIM = 128
BLK = 256
GROUP = 4
MESH = pl.DeviceIdType.MESH


def kernel(
    sizes,
    q_hbm,
    k_hbm,
    v_hbm,
    rate_ref,
    gain_ref,
    out_ref,
    q_buf,
    k_buf,
    v_buf,
    att,
    first_term,
    s_own,
    s_in,
    t_own,
    t_in,
    total,
    f_in,
    b_in,
    pz_out,
    pz_in,
    px_out,
    before,
    sq_own,
    sq_in,
    load_sem,
    s_sem,
    t_sem,
    f_sem,
    b_sem,
    pz_sem,
    px_sem,
    sq_sem,
):
    nz, nx, nt = sizes
    groups = nz // GROUP
    forward, backward = groups // 2, groups - 1 - groups // 2
    rows = q_hbm.shape[0]
    blocks = rows // BLK
    span = rows
    slab = HEAD_DIM // GROUP
    f32, bf16 = jnp.float32, jnp.bfloat16

    z, x, t = lax.axis_index("ctx"), lax.axis_index("exp"), lax.axis_index("tp")
    low = lax.rem(z, GROUP)
    high = lax.div(z, GROUP)

    def x_at(k):
        return lax.rem(x + (k + nx), nx)

    def low_at(k):
        return lax.rem(low + (k + GROUP), GROUP)

    def z_at(k):
        return z - low + low_at(k)

    def t_at(k):
        return lax.rem(t + k, nt)

    z_up, z_down = lax.rem(z + GROUP, nz), lax.rem(z + nz - GROUP, nz)

    barrier = pltpu.get_barrier_semaphore()
    for k in range(1, GROUP):
        pl.semaphore_signal(barrier, inc=1, device_id={"ctx": z_at(k)}, device_id_type=MESH)
    pl.semaphore_signal(barrier, inc=1, device_id={"ctx": z_up}, device_id_type=MESH)
    pl.semaphore_signal(barrier, inc=1, device_id={"ctx": z_down}, device_id_type=MESH)
    for k in range(1, nx):
        pl.semaphore_signal(barrier, inc=1, device_id={"exp": x_at(k)}, device_id_type=MESH)
    for k in range(1, nt):
        pl.semaphore_signal(barrier, inc=1, device_id={"tp": t_at(k)}, device_id_type=MESH)

    def load(which, slot):
        source, target = ((k_hbm, k_buf), (v_hbm, v_buf), (q_hbm, q_buf))[which]
        lanes = pl.ds(pl.multiple_of(x_at(slot) * HEAD_DIM, HEAD_DIM), HEAD_DIM)
        return pltpu.make_async_copy(
            source.at[:, lanes], target.at[slot], load_sem.at[which, slot]
        )

    order = [2, 1, 3, 0] if nx == 4 else list(range(1, nx)) + [0]
    for slot in order:
        load(0, slot).start()
        load(1, slot).start()
    for slot in range(nx):
        load(2, slot).start()

    def rate_of(slot):
        return rate_ref[x_at(slot)]

    def decay(rate, distance, valid=None):
        distance = jnp.maximum(distance, 0)
        weight = jnp.exp(jnp.full((1, HEAD_DIM), -rate * distance.astype(f32), f32))
        if valid is not None:
            weight = weight * jnp.where(valid, 1.0, 0.0).astype(f32)
        return weight

    def fixed_decay(rate, distance):
        return jnp.exp(jnp.full((1, HEAD_DIM), -rate * float(distance), f32))

    def send_s(k):
        return pltpu.make_async_remote_copy(
            s_own.at[k], s_in.at[k - 1], s_sem.at[0, k - 1], s_sem.at[1, k - 1],
            device_id={"exp": x_at(k)}, device_id_type=MESH,
        )

    def send_t(k):
        return pltpu.make_async_remote_copy(
            t_own.at[low_at(k)], t_in.at[k - 1], t_sem.at[0, k - 1], t_sem.at[1, k - 1],
            device_id={"ctx": z_at(k)}, device_id_type=MESH,
        )

    def send_f(s):
        return pltpu.make_async_remote_copy(
            total if s == 0 else f_in.at[s - 1], f_in.at[s], f_sem.at[0, s], f_sem.at[1, s],
            device_id={"ctx": z_up}, device_id_type=MESH,
        )

    def send_b(s):
        return pltpu.make_async_remote_copy(
            total if s == 0 else b_in.at[s - 1], b_in.at[s], b_sem.at[0, s], b_sem.at[1, s],
            device_id={"ctx": z_down}, device_id_type=MESH,
        )

    def send_pz(k):
        return pltpu.make_async_remote_copy(
            pz_out.at[k], pz_in.at[k - 1], pz_sem.at[0, k - 1], pz_sem.at[1, k - 1],
            device_id={"ctx": z_at(k)}, device_id_type=MESH,
        )

    def send_px(q, k):
        return pltpu.make_async_remote_copy(
            px_out.at[q - 1, k], before.at[nx - q, low_at(-k)],
            px_sem.at[0, q - 1, k], px_sem.at[1, q - 1, k],
            device_id={"exp": x_at(q)}, device_id_type=MESH,
        )

    def send_sq(k):
        return pltpu.make_async_remote_copy(
            sq_own, sq_in.at[k - 1], sq_sem.at[0, k - 1], sq_sem.at[1, k - 1],
            device_id={"tp": t_at(k)}, device_id_type=MESH,
        )

    position = lax.broadcasted_iota(jnp.int32, (BLK, HEAD_DIM), 0).astype(f32)
    entered = False
    for slot in order:
        rate = rate_of(slot)
        load(0, slot).wait()
        load(1, slot).wait()
        tail = jnp.exp(-rate * (BLK - position))
        block_decay = fixed_decay(rate, BLK)
        state = None
        for block in range(blocks):
            at = pl.ds(block * BLK, BLK)
            scaled = (k_buf[slot, at, :].astype(f32) * tail).astype(bf16)
            term = lax.dot_general(
                scaled, v_buf[slot, at, :], (((0,), (0,)), ((), ())), preferred_element_type=f32
            )
            if block < blocks - 1:
                first_term[slot, block] = term
            state = term if state is None else block_decay * state + term
        s_own[slot] = state
        if not entered:
            pl.semaphore_wait(barrier, (GROUP - 1) + 2 + (nx - 1) + (nt - 1))
            entered = True
        if slot != 0:
            send_s(slot).start()

    rate = rate_of(0)
    x_weight = [decay(rate, span * (nx - 1 - x_at(-k))) for k in range(nx)]
    plane = x_weight[0] * s_own[0]
    for k in range(1, nx):
        send_s(k).wait_recv()
        plane = plane + x_weight[k] * s_in[k - 1]
    for i in range(GROUP):
        t_own[i] = plane[i * slab : (i + 1) * slab]
    for k in (3, 2, 1):
        send_t(k).start()
    z_span = span * nx
    z_weight = [decay(rate, z_span * (GROUP - 1 - low_at(-k))) for k in range(GROUP)]
    whole = z_weight[0] * t_own[low]
    for k in range(1, GROUP):
        send_t(k).wait_recv()
        whole = whole + z_weight[k] * t_in[k - 1]
    total[...] = whole
    send_f(0).start()
    if backward:
        send_b(0).start()

    line = lax.broadcasted_iota(jnp.int32, (BLK, BLK), 0)
    column = lax.broadcasted_iota(jnp.int32, (BLK, BLK), 1)
    causal = line >= column
    spread = jnp.maximum(line - column, 0).astype(f32)

    def mix(slot):
        load(2, slot).wait()
        weight = jnp.where(causal, jnp.exp(-rate_of(slot) * spread), 0.0)
        for block in range(blocks):
            at = pl.ds(block * BLK, BLK)
            scores = lax.dot_general(
                q_buf[slot, at, :], k_buf[slot, at, :], (((1,), (1,)), ((), ())),
                preferred_element_type=f32,
            )
            mixing = (scores * weight).astype(bf16)
            att[slot, at, :] = jnp.dot(mixing, v_buf[slot, at, :], preferred_element_type=f32)

    group_span = z_span * GROUP
    pending = list(range(nx))
    for s in range(forward):
        take = -(-len(pending) // (forward - s))
        for slot in pending[:take]:
            mix(slot)
        pending = pending[take:]
        send_f(s).wait_recv()
        if s + 1 < forward:
            send_f(s + 1).start()
        if s < backward:
            send_b(s).wait_recv()
            if s + 1 < backward:
                send_b(s + 1).start()

    incoming = jnp.zeros((slab, HEAD_DIM), f32)
    for s in range(forward):
        incoming = incoming + decay(rate, jnp.int32(group_span * s), high - (s + 1) >= 0) * f_in[s]
    for s in range(backward):
        far = jnp.int32(group_span * (groups - 2 - s))
        incoming = incoming + decay(rate, far, high + (s + 1) - groups >= 0) * b_in[s]

    slabs = [t_own[low]] + [t_in[k - 1] for k in range(1, GROUP)]
    for k in (3, 2, 1, 0):
        goal = low_at(k)
        value = decay(rate, z_span * goal) * incoming
        for j in range(GROUP):
            source = low_at(-j)
            value = value + decay(rate, z_span * (goal - 1 - source), source < goal) * slabs[j]
        pz_out[k] = value
        if k:
            send_pz(k).start()

    weights = []
    for q in range(nx):
        goal = x_at(q)
        weights.append(
            (
                decay(rate, span * goal),
                [
                    decay(rate, span * (goal - 1 - x_at(-j)), x_at(-j) < goal)
                    for j in range(nx)
                ],
            )
        )
    for k in range(GROUP):
        if k:
            send_pz(k).wait_recv()
            base = pz_in[k - 1]
        else:
            base = pz_out[0]
        index = low_at(-k)
        at = pl.ds(pl.multiple_of(index * slab, slab), slab)
        terms = [s_own[0, at, :]] + [s_in[j - 1, at, :] for j in range(1, nx)]
        for q in (2, 1, 3, 0) if nx == 4 else tuple(range(1, nx)) + (0,):
            entry, inner = weights[q]
            value = entry * base
            for j in range(nx):
                value = value + inner[j] * terms[j]
            if q:
                px_out[q - 1, k] = value
                send_px(q, k).start()
            else:
                before[0, index] = value

    squares = [jnp.zeros((BLK, HEAD_DIM), f32) for block in range(blocks)]
    for q in range(nx):
        slot = (nx - q) % nx
        if q:
            for k in range(GROUP):
                pltpu.make_async_remote_copy(
                    px_out.at[q - 1, k], before.at[slot, low_at(-k)],
                    px_sem.at[0, q - 1, k], px_sem.at[1, q - 1, k],
                    device_id={"exp": x_at(q)}, device_id_type=MESH,
                ).wait_recv()
        rate = rate_of(slot)
        inner_decay = jnp.exp(-rate * position)
        block_decay = fixed_decay(rate, BLK)
        state = before[slot].reshape(HEAD_DIM, HEAD_DIM)
        for block in range(blocks):
            at = pl.ds(block * BLK, BLK)
            carried = jnp.dot(
                q_buf[slot, at, :], state.astype(bf16), preferred_element_type=f32
            )
            attended = att[slot, at, :] + carried * inner_decay
            att[slot, at, :] = attended
            squares[block] = squares[block] + attended * attended
            if block < blocks - 1:
                state = block_decay * state + first_term[slot, block]

    pieces = rows // HEAD_DIM
    per_block = BLK // HEAD_DIM
    for c in range(pieces):
        part = squares[c // per_block][(c % per_block) * HEAD_DIM : (c % per_block + 1) * HEAD_DIM]
        sq_own[pl.ds(c, 1), :] = jnp.sum(part.T, axis=0, keepdims=True)
    for k in range(1, nt):
        send_sq(k).start()
    sum_squares = sq_own[...]
    for k in range(1, nt):
        send_sq(k).wait_recv()
        sum_squares = sum_squares + sq_in[k - 1]
    scale = lax.rsqrt(sum_squares / (nt * nx * HEAD_DIM) + 1e-06)
    for c in range(pieces):
        at = pl.ds(c * HEAD_DIM, HEAD_DIM)
        row_scale = jnp.broadcast_to(scale[c : c + 1], (HEAD_DIM, HEAD_DIM)).T
        for slot in range(nx):
            head = x_at(slot)
            lanes = pl.ds(pl.multiple_of(head * HEAD_DIM, HEAD_DIM), HEAD_DIM)
            gain = gain_ref[pl.ds(head, 1), :]
            out_ref[at, lanes] = (att[slot, at, :] * row_scale * gain).astype(bf16)

    for k in range(1, nx):
        send_s(k).wait_send()
        for c in range(GROUP):
            send_px(k, c).wait_send()
    for k in range(1, GROUP):
        send_t(k).wait_send()
        send_pz(k).wait_send()
    for s in range(forward):
        send_f(s).wait_send()
    for s in range(backward):
        send_b(s).wait_send()
    for k in range(1, nt):
        send_sq(k).wait_send()


def solution(mesh):
    nz, nx, nt = mesh.shape["ctx"], mesh.shape["exp"], mesh.shape["tp"]
    groups = nz // GROUP
    forward, backward = groups // 2, groups - 1 - groups // 2
    slab = HEAD_DIM // GROUP

    def local(queries, key_vectors, value_vectors, decay_rate, norm_gain):
        rows, width = queries.shape
        heads = width // HEAD_DIM
        blocks = rows // BLK
        f32 = jnp.float32
        square = (HEAD_DIM, HEAD_DIM)
        piece = (slab, HEAD_DIM)
        dma = pltpu.SemaphoreType.DMA
        scratch = [
            pltpu.VMEM((heads, rows, HEAD_DIM), jnp.bfloat16),
            pltpu.VMEM((heads, rows, HEAD_DIM), jnp.bfloat16),
            pltpu.VMEM((heads, rows, HEAD_DIM), jnp.bfloat16),
            pltpu.VMEM((heads, rows, HEAD_DIM), f32),
            pltpu.VMEM((heads, max(blocks - 1, 1)) + square, f32),
            pltpu.VMEM((heads,) + square, f32),
            pltpu.VMEM((nx - 1,) + square, f32),
            pltpu.VMEM((GROUP,) + piece, f32),
            pltpu.VMEM((GROUP - 1,) + piece, f32),
            pltpu.VMEM(piece, f32),
            pltpu.VMEM((forward,) + piece, f32),
            pltpu.VMEM((max(backward, 1),) + piece, f32),
            pltpu.VMEM((GROUP,) + piece, f32),
            pltpu.VMEM((GROUP - 1,) + piece, f32),
            pltpu.VMEM((nx - 1, GROUP) + piece, f32),
            pltpu.VMEM((heads, GROUP) + piece, f32),
            pltpu.VMEM((rows // HEAD_DIM, HEAD_DIM), f32),
            pltpu.VMEM((nt - 1, rows // HEAD_DIM, HEAD_DIM), f32),
            dma((3, heads)),
            dma((2, nx - 1)),
            dma((2, GROUP - 1)),
            dma((2, forward)),
            dma((2, max(backward, 1))),
            dma((2, GROUP - 1)),
            dma((2, nx - 1, GROUP)),
            dma((2, nt - 1)),
        ]
        return pl.pallas_call(
            functools.partial(kernel, (nz, nx, nt)),
            out_shape=jax.ShapeDtypeStruct((rows, width), jnp.bfloat16),
            in_specs=[
                pl.BlockSpec(memory_space=pl.ANY),
                pl.BlockSpec(memory_space=pl.ANY),
                pl.BlockSpec(memory_space=pl.ANY),
                pl.BlockSpec(memory_space=pltpu.SMEM),
                pl.BlockSpec(memory_space=pltpu.VMEM),
            ],
            out_specs=pl.BlockSpec(memory_space=pltpu.VMEM),
            scratch_shapes=scratch,
            compiler_params=pltpu.CompilerParams(collective_id=0, has_side_effects=True),
            name="lightning",
        )(queries, key_vectors, value_vectors, decay_rate, norm_gain.reshape(heads, HEAD_DIM))

    return jax.shard_map(
        local,
        mesh=mesh,
        in_specs=(
            P(("ctx", "exp"), "tp"),
            P(("ctx", "exp"), "tp"),
            P(("ctx", "exp"), "tp"),
            P("tp"),
            P("tp"),
        ),
        out_specs=P(("ctx", "exp"), "tp"),
        check_vma=False,
    )
```

time: 573 us -> 68.4 us (0.12)
  blocking collectives: 254 us -> 0 us
  waiting for transfers between devices: 150 us -> 0 us
  other arithmetic: 136 us -> 0 us
  Pallas kernels: 0 us -> 66.3 us
  between operations: 14.2 us -> 0.01 us
  local copies, waits for them, and re-layouts: 7.91 us -> 1.87 us
    unnamed x1 -> x0, blocking collectives: 241 us -> none
    all_gather x1 -> x0, waiting for transfers between devices: 150 us -> none  [carried_in(): pieces = jax.tree.map(lambda part: lax.all_gather(part, axis), value)]
    select_n x127 -> x0, other arithmetic: 134 us -> none  [hop(): jnp.where(position < mine, new, old)]
    pallas_call x0 -> x1, Pallas kernels: none -> 66.3 us  [local(): pl.pallas_call(functools.partial(kernel, (nz, nx, nt)), out_shape=jax.Sha...]
    psum x1 -> x0, blocking collectives: 13.2 us -> none  [local(): row_total = lax.psum(row_squares, 'tp')]
  transfers between devices with their start and end apart: 1 -> 0, of which waited for: 1 -> 0; matrix products, arithmetic and copies ran while one was open for 0% -> 0% of each run, Pallas kernels for 0% -> 0%
where the time goes in v1:
time: 68.4 us; the launch traced here: 68.1 us
  Pallas kernels  66.3 us (97%)
  local copies, waits for them, and re-layouts  1.87 us (3%)
    pallas_call x1, Pallas kernels, local(): pl.pallas_call(functools.partial(kernel, (nz, nx, nt)), out_shape=jax.Sha...  66.3 us
    unnamed x1, local copies, waits for them, and re-layouts  1.87 us

profile of v1, /device:TPU:1, one launch (start us, length us, event | category | flops | bytes accessed | tf_op | source)
XLA Modules:
  0.0 68.1 jit_solution(14363578056028321753)
XLA Ops:
  0.0 66.3 %lightning.1 = bf16[512,512]{1,0:T(8,128)(2,1)} custom-call(bf16[512,512]{1,0:T(8,128)(2,1)} %q_hbm.1, bf16[512,512]{1,0:T(8,128)(2,1)} %k_hbm.1, bf16[512,512]{1,0:T(8,128)(2,1)} %v_hbm.1, f32[4]{0:T(128)} %rate_ref.1, f32[4,128]{1,0:T(4,128)} %bitcast.1), custom_call_target="tpu_custom_call" | custom-call | tf_op jit(solution)/shard_map/lightning/pallas_call | solution.py:390
  66.3 1.9 %copy.7 = bf16[512,512]{1,0:T(8,128)(2,1)} copy(bf16[512,512]{1,0:T(8,128)(2,1)} %lightning.1) | data formatting | bytes 1048576

commit v2 on v1

--- a/solution.py
+++ b/solution.py
@@ -31,9 +31,8 @@
     s_in,
     t_own,
     t_in,
-    total,
-    f_in,
-    b_in,
+    up_out,
+    up_in,
     pz_out,
     pz_in,
     px_out,
@@ -43,15 +42,13 @@
     load_sem,
     s_sem,
     t_sem,
-    f_sem,
-    b_sem,
+    up_sem,
     pz_sem,
     px_sem,
     sq_sem,
 ):
     nz, nx, nt = sizes
     groups = nz // GROUP
-    forward, backward = groups // 2, groups - 1 - groups // 2
     rows = q_hbm.shape[0]
     blocks = rows // BLK
     span = rows
@@ -75,12 +72,16 @@
         return lax.rem(t + k, nt)
 
     z_up, z_down = lax.rem(z + GROUP, nz), lax.rem(z + nz - GROUP, nz)
+    has_up = high < groups - 1
 
     barrier = pltpu.get_barrier_semaphore()
     for k in range(1, GROUP):
         pl.semaphore_signal(barrier, inc=1, device_id={"ctx": z_at(k)}, device_id_type=MESH)
-    pl.semaphore_signal(barrier, inc=1, device_id={"ctx": z_up}, device_id_type=MESH)
-    pl.semaphore_signal(barrier, inc=1, device_id={"ctx": z_down}, device_id_type=MESH)
+
+    @pl.when(high > 0)
+    def _():
+        pl.semaphore_signal(barrier, inc=1, device_id={"ctx": z_down}, device_id_type=MESH)
+
     for k in range(1, nx):
         pl.semaphore_signal(barrier, inc=1, device_id={"exp": x_at(k)}, device_id_type=MESH)
     for k in range(1, nt):
@@ -113,28 +114,23 @@
     def fixed_decay(rate, distance):
         return jnp.exp(jnp.full((1, HEAD_DIM), -rate * float(distance), f32))
 
-    def send_s(k):
-        return pltpu.make_async_remote_copy(
-            s_own.at[k], s_in.at[k - 1], s_sem.at[0, k - 1], s_sem.at[1, k - 1],
+    def send_s(k, o):
+        return pltpu.make_async_remote_copy(
+            s_own.at[k, low_at(o)], s_in.at[k - 1, low_at(o)],
+            s_sem.at[0, k - 1, o], s_sem.at[1, k - 1, o],
             device_id={"exp": x_at(k)}, device_id_type=MESH,
         )
 
     def send_t(k):
         return pltpu.make_async_remote_copy(
-            t_own.at[low_at(k)], t_in.at[k - 1], t_sem.at[0, k - 1], t_sem.at[1, k - 1],
+            t_own.at[k], t_in.at[k - 1], t_sem.at[0, k - 1], t_sem.at[1, k - 1],
             device_id={"ctx": z_at(k)}, device_id_type=MESH,
         )
 
-    def send_f(s):
-        return pltpu.make_async_remote_copy(
-            total if s == 0 else f_in.at[s - 1], f_in.at[s], f_sem.at[0, s], f_sem.at[1, s],
+    def send_up():
+        return pltpu.make_async_remote_copy(
+            up_out, up_in, up_sem.at[0], up_sem.at[1],
             device_id={"ctx": z_up}, device_id_type=MESH,
-        )
-
-    def send_b(s):
-        return pltpu.make_async_remote_copy(
-            total if s == 0 else b_in.at[s - 1], b_in.at[s], b_sem.at[0, s], b_sem.at[1, s],
-            device_id={"ctx": z_down}, device_id_type=MESH,
         )
 
     def send_pz(k):
@@ -174,40 +170,28 @@
             if block < blocks - 1:
                 first_term[slot, block] = term
             state = term if state is None else block_decay * state + term
-        s_own[slot] = state
+        s_own[slot] = state.reshape(GROUP, slab, HEAD_DIM)
         if not entered:
-            pl.semaphore_wait(barrier, (GROUP - 1) + 2 + (nx - 1) + (nt - 1))
+            partners = (GROUP - 1) + (nx - 1) + (nt - 1)
+
+            @pl.when(has_up)
+            def _():
+                pl.semaphore_wait(barrier, partners + 1)
+
+            @pl.when(jnp.logical_not(has_up))
+            def _():
+                pl.semaphore_wait(barrier, partners)
+
             entered = True
         if slot != 0:
-            send_s(slot).start()
-
-    rate = rate_of(0)
-    x_weight = [decay(rate, span * (nx - 1 - x_at(-k))) for k in range(nx)]
-    plane = x_weight[0] * s_own[0]
-    for k in range(1, nx):
-        send_s(k).wait_recv()
-        plane = plane + x_weight[k] * s_in[k - 1]
-    for i in range(GROUP):
-        t_own[i] = plane[i * slab : (i + 1) * slab]
-    for k in (3, 2, 1):
-        send_t(k).start()
-    z_span = span * nx
-    z_weight = [decay(rate, z_span * (GROUP - 1 - low_at(-k))) for k in range(GROUP)]
-    whole = z_weight[0] * t_own[low]
-    for k in range(1, GROUP):
-        send_t(k).wait_recv()
-        whole = whole + z_weight[k] * t_in[k - 1]
-    total[...] = whole
-    send_f(0).start()
-    if backward:
-        send_b(0).start()
+            for o in (3, 2, 1, 0):
+                send_s(slot, o).start()
 
     line = lax.broadcasted_iota(jnp.int32, (BLK, BLK), 0)
     column = lax.broadcasted_iota(jnp.int32, (BLK, BLK), 1)
     causal = line >= column
     spread = jnp.maximum(line - column, 0).astype(f32)
-
-    def mix(slot):
+    for slot in range(nx):
         load(2, slot).wait()
         weight = jnp.where(causal, jnp.exp(-rate_of(slot) * spread), 0.0)
         for block in range(blocks):
@@ -219,29 +203,39 @@
             mixing = (scores * weight).astype(bf16)
             att[slot, at, :] = jnp.dot(mixing, v_buf[slot, at, :], preferred_element_type=f32)
 
-    group_span = z_span * GROUP
-    pending = list(range(nx))
-    for s in range(forward):
-        take = -(-len(pending) // (forward - s))
-        for slot in pending[:take]:
-            mix(slot)
-        pending = pending[take:]
-        send_f(s).wait_recv()
-        if s + 1 < forward:
-            send_f(s + 1).start()
-        if s < backward:
-            send_b(s).wait_recv()
-            if s + 1 < backward:
-                send_b(s + 1).start()
-
-    incoming = jnp.zeros((slab, HEAD_DIM), f32)
-    for s in range(forward):
-        incoming = incoming + decay(rate, jnp.int32(group_span * s), high - (s + 1) >= 0) * f_in[s]
-    for s in range(backward):
-        far = jnp.int32(group_span * (groups - 2 - s))
-        incoming = incoming + decay(rate, far, high + (s + 1) - groups >= 0) * b_in[s]
-
-    slabs = [t_own[low]] + [t_in[k - 1] for k in range(1, GROUP)]
+    rate = rate_of(0)
+    x_weight = [decay(rate, span * (nx - 1 - x_at(-k))) for k in range(nx)]
+    z_span = span * nx
+    z_weight = [decay(rate, z_span * (GROUP - 1 - low_at(-k))) for k in range(GROUP)]
+    for o in (3, 2, 1, 0):
+        plane = x_weight[0] * s_own[0, low_at(o)]
+        for k in range(1, nx):
+            send_s(k, o).wait_recv()
+            plane = plane + x_weight[k] * s_in[k - 1, low_at(o)]
+        t_own[o] = plane
+        if o:
+            send_t(o).start()
+    whole = z_weight[0] * t_own[0]
+    for k in range(1, GROUP):
+        send_t(k).wait_recv()
+        whole = whole + z_weight[k] * t_in[k - 1]
+
+    @pl.when(high > 0)
+    def _():
+        send_up().wait_recv()
+
+    @pl.when(high == 0)
+    def _():
+        up_in[...] = jnp.zeros_like(up_in)
+
+    incoming = up_in[...]
+
+    @pl.when(has_up)
+    def _():
+        up_out[...] = whole + fixed_decay(rate, z_span * GROUP) * incoming
+        send_up().start()
+
+    slabs = [t_own[0]] + [t_in[k - 1] for k in range(1, GROUP)]
     for k in (3, 2, 1, 0):
         goal = low_at(k)
         value = decay(rate, z_span * goal) * incoming
@@ -271,8 +265,7 @@
         else:
             base = pz_out[0]
         index = low_at(-k)
-        at = pl.ds(pl.multiple_of(index * slab, slab), slab)
-        terms = [s_own[0, at, :]] + [s_in[j - 1, at, :] for j in range(1, nx)]
+        terms = [s_own[0, index]] + [s_in[j - 1, index] for j in range(1, nx)]
         for q in (2, 1, 3, 0) if nx == 4 else tuple(range(1, nx)) + (0,):
             entry, inner = weights[q]
             value = entry * base
@@ -331,24 +324,23 @@
             out_ref[at, lanes] = (att[slot, at, :] * row_scale * gain).astype(bf16)
 
     for k in range(1, nx):
-        send_s(k).wait_send()
         for c in range(GROUP):
+            send_s(k, c).wait_send()
             send_px(k, c).wait_send()
     for k in range(1, GROUP):
         send_t(k).wait_send()
         send_pz(k).wait_send()
-    for s in range(forward):
-        send_f(s).wait_send()
-    for s in range(backward):
-        send_b(s).wait_send()
+
+    @pl.when(has_up)
+    def _():
+        send_up().wait_send()
+
     for k in range(1, nt):
         send_sq(k).wait_send()
 
 
 def solution(mesh):
     nz, nx, nt = mesh.shape["ctx"], mesh.shape["exp"], mesh.shape["tp"]
-    groups = nz // GROUP
-    forward, backward = groups // 2, groups - 1 - groups // 2
     slab = HEAD_DIM // GROUP
 
     def local(queries, key_vectors, value_vectors, decay_rate, norm_gain):
@@ -365,13 +357,12 @@
             pltpu.VMEM((heads, rows, HEAD_DIM), jnp.bfloat16),
             pltpu.VMEM((heads, rows, HEAD_DIM), f32),
             pltpu.VMEM((heads, max(blocks - 1, 1)) + square, f32),
-            pltpu.VMEM((heads,) + square, f32),
-            pltpu.VMEM((nx - 1,) + square, f32),
+            pltpu.VMEM((heads, GROUP) + piece, f32),
+            pltpu.VMEM((nx - 1, GROUP) + piece, f32),
             pltpu.VMEM((GROUP,) + piece, f32),
             pltpu.VMEM((GROUP - 1,) + piece, f32),
             pltpu.VMEM(piece, f32),
-            pltpu.VMEM((forward,) + piece, f32),
-            pltpu.VMEM((max(backward, 1),) + piece, f32),
+            pltpu.VMEM(piece, f32),
             pltpu.VMEM((GROUP,) + piece, f32),
             pltpu.VMEM((GROUP - 1,) + piece, f32),
             pltpu.VMEM((nx - 1, GROUP) + piece, f32),
@@ -379,10 +370,9 @@
             pltpu.VMEM((rows // HEAD_DIM, HEAD_DIM), f32),
             pltpu.VMEM((nt - 1, rows // HEAD_DIM, HEAD_DIM), f32),
             dma((3, heads)),
-            dma((2, nx - 1)),
+            dma((2, nx - 1, GROUP)),
             dma((2, GROUP - 1)),
-            dma((2, forward)),
-            dma((2, max(backward, 1))),
+            dma((2,)),
             dma((2, GROUP - 1)),
             dma((2, nx - 1, GROUP)),
             dma((2, nt - 1)),

time: 68.4 us -> 57.9 us (0.85)
  the two profiles are of different devices: /device:TPU:1 before, /device:TPU:897 now
where the time goes in v2:
time: 57.9 us; the launch traced here: 57.7 us
  Pallas kernels  55.8 us (96%)
  local copies, waits for them, and re-layouts  1.87 us (3%)
    pallas_call x1, Pallas kernels, local(): pl.pallas_call(functools.partial(kernel, (nz, nx, nt)), out_shape=jax.Sha...  55.8 us
    unnamed x1, local copies, waits for them, and re-layouts  1.87 us

profile of v2, /device:TPU:897, one launch (start us, length us, event | category | flops | bytes accessed | tf_op | source)
XLA Modules:
  0.0 57.7 jit_solution(9389143066245172431)
XLA Ops:
  0.0 55.8 %lightning.1 = bf16[512,512]{1,0:T(8,128)(2,1)} custom-call(bf16[512,512]{1,0:T(8,128)(2,1)} %q_hbm.1, bf16[512,512]{1,0:T(8,128)(2,1)} %k_hbm.1, bf16[512,512]{1,0:T(8,128)(2,1)} %v_hbm.1, f32[4]{0:T(128)} %rate_ref.1, f32[4,128]{1,0:T(4,128)} %bitcast.1), custom_call_target="tpu_custom_call" | custom-call | tf_op jit(solution)/shard_map/lightning/pallas_call | solution.py:380
  55.8 1.9 %copy.7 = bf16[512,512]{1,0:T(8,128)(2,1)} copy(bf16[512,512]{1,0:T(8,128)(2,1)} %lightning.1) | data formatting | bytes 1048576

commit v3 on v2

--- a/solution.py
+++ b/solution.py
@@ -19,9 +19,11 @@
     q_hbm,
     k_hbm,
     v_hbm,
+    rate_hbm,
+    gain_hbm,
+    out_ref,
     rate_ref,
     gain_ref,
-    out_ref,
     q_buf,
     k_buf,
     v_buf,
@@ -40,6 +42,10 @@
     sq_own,
     sq_in,
     load_sem,
+    rate_sem,
+    gain_sem,
+    below_sem,
+    above_sem,
     s_sem,
     t_sem,
     up_sem,
@@ -78,9 +84,16 @@
     for k in range(1, GROUP):
         pl.semaphore_signal(barrier, inc=1, device_id={"ctx": z_at(k)}, device_id_type=MESH)
 
-    @pl.when(high > 0)
-    def _():
-        pl.semaphore_signal(barrier, inc=1, device_id={"ctx": z_down}, device_id_type=MESH)
+    top = jnp.logical_and(low == GROUP - 1, has_up)
+    bottom = jnp.logical_and(low == 0, high > 0)
+
+    @pl.when(top)
+    def _():
+        pl.semaphore_signal(barrier, inc=1, device_id={"ctx": z + 1}, device_id_type=MESH)
+
+    @pl.when(bottom)
+    def _():
+        pl.semaphore_signal(barrier, inc=1, device_id={"ctx": z - 1}, device_id_type=MESH)
 
     for k in range(1, nx):
         pl.semaphore_signal(barrier, inc=1, device_id={"exp": x_at(k)}, device_id_type=MESH)
@@ -94,12 +107,16 @@
             source.at[:, lanes], target.at[slot], load_sem.at[which, slot]
         )
 
+    rate_copy = pltpu.make_async_copy(rate_hbm, rate_ref, rate_sem)
+    gain_copy = pltpu.make_async_copy(gain_hbm, gain_ref, gain_sem)
+    rate_copy.start()
     order = [2, 1, 3, 0] if nx == 4 else list(range(1, nx)) + [0]
     for slot in order:
         load(0, slot).start()
         load(1, slot).start()
     for slot in range(nx):
         load(2, slot).start()
+    gain_copy.start()
 
     def rate_of(slot):
         return rate_ref[x_at(slot)]
@@ -154,6 +171,7 @@
 
     position = lax.broadcasted_iota(jnp.int32, (BLK, HEAD_DIM), 0).astype(f32)
     entered = False
+    rate_copy.wait()
     for slot in order:
         rate = rate_of(slot)
         load(0, slot).wait()
@@ -174,11 +192,13 @@
         if not entered:
             partners = (GROUP - 1) + (nx - 1) + (nt - 1)
 
-            @pl.when(has_up)
+            edge = jnp.logical_or(top, bottom)
+
+            @pl.when(edge)
             def _():
                 pl.semaphore_wait(barrier, partners + 1)
 
-            @pl.when(jnp.logical_not(has_up))
+            @pl.when(jnp.logical_not(edge))
             def _():
                 pl.semaphore_wait(barrier, partners)
 
@@ -186,6 +206,10 @@
         if slot != 0:
             for o in (3, 2, 1, 0):
                 send_s(slot, o).start()
+
+    @pl.when(top)
+    def _():
+        pl.semaphore_signal(below_sem, inc=1, device_id={"ctx": z + 1}, device_id_type=MESH)
 
     line = lax.broadcasted_iota(jnp.int32, (BLK, BLK), 0)
     column = lax.broadcasted_iota(jnp.int32, (BLK, BLK), 1)
@@ -202,6 +226,12 @@
             )
             mixing = (scores * weight).astype(bf16)
             att[slot, at, :] = jnp.dot(mixing, v_buf[slot, at, :], preferred_element_type=f32)
+
+    @pl.when(bottom)
+    def _():
+        pl.semaphore_wait(below_sem, 1)
+        for k in range(1, GROUP + 1):
+            pl.semaphore_signal(above_sem, inc=1, device_id={"ctx": z - k}, device_id_type=MESH)
 
     rate = rate_of(0)
     x_weight = [decay(rate, span * (nx - 1 - x_at(-k))) for k in range(nx)]
@@ -232,6 +262,7 @@
 
     @pl.when(has_up)
     def _():
+        pl.semaphore_wait(above_sem, 1)
         up_out[...] = whole + fixed_decay(rate, z_span * GROUP) * incoming
         send_up().start()
 
@@ -313,6 +344,7 @@
     for k in range(1, nt):
         send_sq(k).wait_recv()
         sum_squares = sum_squares + sq_in[k - 1]
+    gain_copy.wait()
     scale = lax.rsqrt(sum_squares / (nt * nx * HEAD_DIM) + 1e-06)
     for c in range(pieces):
         at = pl.ds(c * HEAD_DIM, HEAD_DIM)
@@ -352,6 +384,8 @@
         piece = (slab, HEAD_DIM)
         dma = pltpu.SemaphoreType.DMA
         scratch = [
+            pltpu.SMEM((heads,), f32),
+            pltpu.VMEM((heads, HEAD_DIM), f32),
             pltpu.VMEM((heads, rows, HEAD_DIM), jnp.bfloat16),
             pltpu.VMEM((heads, rows, HEAD_DIM), jnp.bfloat16),
             pltpu.VMEM((heads, rows, HEAD_DIM), jnp.bfloat16),
@@ -370,6 +404,10 @@
             pltpu.VMEM((rows // HEAD_DIM, HEAD_DIM), f32),
             pltpu.VMEM((nt - 1, rows // HEAD_DIM, HEAD_DIM), f32),
             dma((3, heads)),
+            dma,
+            dma,
+            pltpu.SemaphoreType.REGULAR,
+            pltpu.SemaphoreType.REGULAR,
             dma((2, nx - 1, GROUP)),
             dma((2, GROUP - 1)),
             dma((2,)),
@@ -379,13 +417,13 @@
         ]
         return pl.pallas_call(
             functools.partial(kernel, (nz, nx, nt)),
-            out_shape=jax.ShapeDtypeStruct((rows, width), jnp.bfloat16),
+            out_shape=pltpu.VMEM((rows, width), jnp.bfloat16),
             in_specs=[
                 pl.BlockSpec(memory_space=pl.ANY),
                 pl.BlockSpec(memory_space=pl.ANY),
                 pl.BlockSpec(memory_space=pl.ANY),
-                pl.BlockSpec(memory_space=pltpu.SMEM),
-                pl.BlockSpec(memory_space=pltpu.VMEM),
+                pl.BlockSpec(memory_space=pl.ANY),
+                pl.BlockSpec(memory_space=pl.ANY),
             ],
             out_specs=pl.BlockSpec(memory_space=pltpu.VMEM),
             scratch_shapes=scratch,

time: 57.9 us -> 55.3 us (0.955)
  Pallas kernels: 55.8 us -> 54.4 us
  local copies, waits for them, and re-layouts: 1.87 us -> 0.8 us
    pallas_call x1, Pallas kernels: 55.8 us -> 54.4 us  [local(): pl.pallas_call(functools.partial(kernel, (nz, nx, nt)), out_shape=pltpu.V...]
    unnamed x1, local copies, waits for them, and re-layouts: 1.87 us -> 0.8 us
where the time goes in v3:
time: 55.3 us; the launch traced here: 55.2 us
  Pallas kernels  54.4 us (98%)
  local copies, waits for them, and re-layouts  0.8 us (1%)
    pallas_call x1, Pallas kernels, local(): pl.pallas_call(functools.partial(kernel, (nz, nx, nt)), out_shape=pltpu.V...  54.4 us

profile of v3, /device:TPU:897, one launch (start us, length us, event | category | flops | bytes accessed | tf_op | source)
XLA Modules:
  0.0 55.2 jit_solution(16554397048699541310)
XLA Ops:
  0.0 54.4 %lightning.1 = bf16[512,512]{1,0:T(8,128)(2,1)S(1)} custom-call(bf16[512,512]{1,0:T(8,128)(2,1)} %q_hbm.1, bf16[512,512]{1,0:T(8,128)(2,1)} %k_hbm.1, bf16[512,512]{1,0:T(8,128)(2,1)} %v_hbm.1, f32[4]{0:T(128)} %rate_hbm.1, f32[4,128]{1,0:T(4,128)} %bitcast.1), custom_call_target="tpu_custom_call" | custom-call | tf_op jit(solution)/shard_map/lightning/pallas_call | solution.py:418
  54.4 0.8 %copy.7 = bf16[512,512]{1,0:T(8,128)(2,1)} copy(bf16[512,512]{1,0:T(8,128)(2,1)S(1)} %lightning.1) | data formatting | bytes 1048576

commit v4 on v3

--- a/solution.py
+++ b/solution.py
@@ -35,6 +35,7 @@
     t_in,
     up_out,
     up_in,
+    far_in,
     pz_out,
     pz_in,
     px_out,
@@ -44,8 +45,8 @@
     load_sem,
     rate_sem,
     gain_sem,
-    below_sem,
-    above_sem,
+    up_ok,
+    far_ok,
     s_sem,
     t_sem,
     up_sem,
@@ -77,24 +78,31 @@
     def t_at(k):
         return lax.rem(t + k, nt)
 
-    z_up, z_down = lax.rem(z + GROUP, nz), lax.rem(z + nz - GROUP, nz)
-    has_up = high < groups - 1
+    half = groups // 2
+    odd = lax.rem(high, 2) == 1
+    has_down, has_up = high > 0, high < groups - 1
+    takes_far = jnp.logical_and(odd, high >= half + 1)
+    sends_far = jnp.logical_and(odd, jnp.logical_and(high >= half - 1, high < groups - 2))
+    sends_total = jnp.logical_and(jnp.logical_not(odd), high >= half)
+
+    def z_off(k):
+        return lax.rem(z + (k + nz), nz)
 
     barrier = pltpu.get_barrier_semaphore()
+    partners = (GROUP - 1) + (nx - 1) + (nt - 1)
+
+    @pl.when(sends_far)
+    def _():
+        pl.semaphore_signal(
+            barrier, inc=1, device_id={"ctx": z_off(2 * GROUP)}, device_id_type=MESH
+        )
+
+    @pl.when(has_up)
+    def _():
+        pl.semaphore_signal(barrier, inc=1, device_id={"ctx": z_off(GROUP)}, device_id_type=MESH)
+
     for k in range(1, GROUP):
         pl.semaphore_signal(barrier, inc=1, device_id={"ctx": z_at(k)}, device_id_type=MESH)
-
-    top = jnp.logical_and(low == GROUP - 1, has_up)
-    bottom = jnp.logical_and(low == 0, high > 0)
-
-    @pl.when(top)
-    def _():
-        pl.semaphore_signal(barrier, inc=1, device_id={"ctx": z + 1}, device_id_type=MESH)
-
-    @pl.when(bottom)
-    def _():
-        pl.semaphore_signal(barrier, inc=1, device_id={"ctx": z - 1}, device_id_type=MESH)
-
     for k in range(1, nx):
         pl.semaphore_signal(barrier, inc=1, device_id={"exp": x_at(k)}, device_id_type=MESH)
     for k in range(1, nt):
@@ -147,7 +155,13 @@
     def send_up():
         return pltpu.make_async_remote_copy(
             up_out, up_in, up_sem.at[0], up_sem.at[1],
-            device_id={"ctx": z_up}, device_id_type=MESH,
+            device_id={"ctx": z_off(GROUP)}, device_id_type=MESH,
+        )
+
+    def send_far():
+        return pltpu.make_async_remote_copy(
+            up_out, far_in, up_sem.at[2], up_sem.at[3],
+            device_id={"ctx": z_off(2 * GROUP)}, device_id_type=MESH,
         )
 
     def send_pz(k):
@@ -168,6 +182,28 @@
             sq_own, sq_in.at[k - 1], sq_sem.at[0, k - 1], sq_sem.at[1, k - 1],
             device_id={"tp": t_at(k)}, device_id_type=MESH,
         )
+
+    def enter():
+        @pl.when(jnp.logical_not(has_down))
+        def _():
+            pl.semaphore_wait(barrier, partners)
+
+        @pl.when(jnp.logical_and(has_down, jnp.logical_not(takes_far)))
+        def _():
+            pl.semaphore_wait(barrier, partners + 1)
+
+        @pl.when(takes_far)
+        def _():
+            pl.semaphore_wait(barrier, partners + 2)
+            pl.semaphore_signal(
+                far_ok, inc=1, device_id={"ctx": z_off(-2 * GROUP)}, device_id_type=MESH
+            )
+
+        @pl.when(has_down)
+        def _():
+            pl.semaphore_signal(
+                up_ok, inc=1, device_id={"ctx": z_off(-GROUP)}, device_id_type=MESH
+            )
 
     position = lax.broadcasted_iota(jnp.int32, (BLK, HEAD_DIM), 0).astype(f32)
     entered = False
@@ -190,26 +226,11 @@
             state = term if state is None else block_decay * state + term
         s_own[slot] = state.reshape(GROUP, slab, HEAD_DIM)
         if not entered:
-            partners = (GROUP - 1) + (nx - 1) + (nt - 1)
-
-            edge = jnp.logical_or(top, bottom)
-
-            @pl.when(edge)
-            def _():
-                pl.semaphore_wait(barrier, partners + 1)
-
-            @pl.when(jnp.logical_not(edge))
-            def _():
-                pl.semaphore_wait(barrier, partners)
-
+            enter()
             entered = True
         if slot != 0:
             for o in (3, 2, 1, 0):
                 send_s(slot, o).start()
-
-    @pl.when(top)
-    def _():
-        pl.semaphore_signal(below_sem, inc=1, device_id={"ctx": z + 1}, device_id_type=MESH)
 
     line = lax.broadcasted_iota(jnp.int32, (BLK, BLK), 0)
     column = lax.broadcasted_iota(jnp.int32, (BLK, BLK), 1)
@@ -226,12 +247,6 @@
             )
             mixing = (scores * weight).astype(bf16)
             att[slot, at, :] = jnp.dot(mixing, v_buf[slot, at, :], preferred_element_type=f32)
-
-    @pl.when(bottom)
-    def _():
-        pl.semaphore_wait(below_sem, 1)
-        for k in range(1, GROUP + 1):
-            pl.semaphore_signal(above_sem, inc=1, device_id={"ctx": z - k}, device_id_type=MESH)
 
     rate = rate_of(0)
     x_weight = [decay(rate, span * (nx - 1 - x_at(-k))) for k in range(nx)]
@@ -250,45 +265,77 @@
         send_t(k).wait_recv()
         whole = whole + z_weight[k] * t_in[k - 1]
 
-    @pl.when(high > 0)
+    slabs = [t_own[0]] + [t_in[k - 1] for k in range(1, GROUP)]
+    z_entry = []
+    for k in range(GROUP):
+        goal = low_at(k)
+        z_entry.append(decay(rate, z_span * goal))
+        value = None
+        for j in range(GROUP):
+            if (j + k) % GROUP:
+                source = low_at(-j)
+                term = decay(rate, z_span * (goal - 1 - source), source < goal) * slabs[j]
+                value = term if value is None else value + term
+        pz_out[k] = value
+    x_entry = []
+    for q in range(nx):
+        goal = x_at(q)
+        x_entry.append(decay(rate, span * goal))
+        inner = [decay(rate, span * (goal - 1 - x_at(-j)), x_at(-j) < goal) for j in range(nx)]
+        for k in range(GROUP):
+            index = low_at(-k)
+            value = inner[0] * s_own[0, index]
+            for j in range(1, nx):
+                value = value + inner[j] * s_in[j - 1, index]
+            if q:
+                px_out[q - 1, k] = value
+            else:
+                before[0, index] = value
+    group_decay = fixed_decay(rate, z_span * GROUP)
+
+    @pl.when(has_up)
+    def _():
+        pl.semaphore_wait(up_ok, 1)
+
+    @pl.when(sends_far)
+    def _():
+        pl.semaphore_wait(far_ok, 1)
+
+    @pl.when(sends_total)
+    def _():
+        up_out[...] = whole
+        send_up().start()
+
+    @pl.when(jnp.logical_not(has_down))
+    def _():
+        up_in[...] = jnp.zeros_like(up_in)
+
+    @pl.when(has_down)
     def _():
         send_up().wait_recv()
 
-    @pl.when(high == 0)
-    def _():
-        up_in[...] = jnp.zeros_like(up_in)
+    @pl.when(takes_far)
+    def _():
+        send_far().wait_recv()
+        up_in[...] = up_in[...] + group_decay * far_in[...]
+
+    @pl.when(jnp.logical_and(has_up, jnp.logical_not(sends_total)))
+    def _():
+        up_out[...] = whole + group_decay * up_in[...]
+
+        @pl.when(sends_far)
+        def _():
+            send_far().start()
+
+        send_up().start()
 
     incoming = up_in[...]
 
-    @pl.when(has_up)
-    def _():
-        pl.semaphore_wait(above_sem, 1)
-        up_out[...] = whole + fixed_decay(rate, z_span * GROUP) * incoming
-        send_up().start()
-
-    slabs = [t_own[0]] + [t_in[k - 1] for k in range(1, GROUP)]
     for k in (3, 2, 1, 0):
-        goal = low_at(k)
-        value = decay(rate, z_span * goal) * incoming
-        for j in range(GROUP):
-            source = low_at(-j)
-            value = value + decay(rate, z_span * (goal - 1 - source), source < goal) * slabs[j]
-        pz_out[k] = value
+        pz_out[k] = pz_out[k] + z_entry[k] * incoming
         if k:
             send_pz(k).start()
 
-    weights = []
-    for q in range(nx):
-        goal = x_at(q)
-        weights.append(
-            (
-                decay(rate, span * goal),
-                [
-                    decay(rate, span * (goal - 1 - x_at(-j)), x_at(-j) < goal)
-                    for j in range(nx)
-                ],
-            )
-        )
     for k in range(GROUP):
         if k:
             send_pz(k).wait_recv()
@@ -296,20 +343,15 @@
         else:
             base = pz_out[0]
         index = low_at(-k)
-        terms = [s_own[0, index]] + [s_in[j - 1, index] for j in range(1, nx)]
-        for q in (2, 1, 3, 0) if nx == 4 else tuple(range(1, nx)) + (0,):
-            entry, inner = weights[q]
-            value = entry * base
-            for j in range(nx):
-                value = value + inner[j] * terms[j]
+        for q in (2, 1, 3, 0):
             if q:
-                px_out[q - 1, k] = value
+                px_out[q - 1, k] = px_out[q - 1, k] + x_entry[q] * base
                 send_px(q, k).start()
             else:
-                before[0, index] = value
+                before[0, index] = before[0, index] + x_entry[0] * base
 
     squares = [jnp.zeros((BLK, HEAD_DIM), f32) for block in range(blocks)]
-    for q in range(nx):
+    for q in (0, 1, 3, 2):
         slot = (nx - q) % nx
         if q:
             for k in range(GROUP):
@@ -367,6 +409,10 @@
     def _():
         send_up().wait_send()
 
+    @pl.when(sends_far)
+    def _():
+        send_far().wait_send()
+
     for k in range(1, nt):
         send_sq(k).wait_send()
 
@@ -397,6 +443,7 @@
             pltpu.VMEM((GROUP - 1,) + piece, f32),
             pltpu.VMEM(piece, f32),
             pltpu.VMEM(piece, f32),
+            pltpu.VMEM(piece, f32),
             pltpu.VMEM((GROUP,) + piece, f32),
             pltpu.VMEM((GROUP - 1,) + piece, f32),
             pltpu.VMEM((nx - 1, GROUP) + piece, f32),
@@ -410,7 +457,7 @@
             pltpu.SemaphoreType.REGULAR,
             dma((2, nx - 1, GROUP)),
             dma((2, GROUP - 1)),
-            dma((2,)),
+            dma((4,)),
             dma((2, GROUP - 1)),
             dma((2, nx - 1, GROUP)),
             dma((2, nt - 1)),

time: 55.3 us -> 50.8 us (0.919)
  Pallas kernels: 54.4 us -> 49.9 us
    pallas_call x1, Pallas kernels: 54.4 us -> 49.9 us  [local(): pl.pallas_call(functools.partial(kernel, (nz, nx, nt)), out_shape=pltpu.V...]
where the time goes in v4:
time: 50.8 us; the launch traced here: 50.7 us
  Pallas kernels  49.9 us (98%)
  local copies, waits for them, and re-layouts  0.8 us (2%)
    pallas_call x1, Pallas kernels, local(): pl.pallas_call(functools.partial(kernel, (nz, nx, nt)), out_shape=pltpu.V...  49.9 us

profile of v4, /device:TPU:897, one launch (start us, length us, event | category | flops | bytes accessed | tf_op | source)
XLA Modules:
  0.0 50.7 jit_solution(2184779443188275941)
XLA Ops:
  0.0 49.9 %lightning.1 = bf16[512,512]{1,0:T(8,128)(2,1)S(1)} custom-call(bf16[512,512]{1,0:T(8,128)(2,1)} %q_hbm.1, bf16[512,512]{1,0:T(8,128)(2,1)} %k_hbm.1, bf16[512,512]{1,0:T(8,128)(2,1)} %v_hbm.1, f32[4]{0:T(128)} %rate_hbm.1, f32[4,128]{1,0:T(4,128)} %bitcast.1), custom_call_target="tpu_custom_call" | custom-call | tf_op jit(solution)/shard_map/lightning/pallas_call | solution.py:465
  49.9 0.8 %copy.7 = bf16[512,512]{1,0:T(8,128)(2,1)} copy(bf16[512,512]{1,0:T(8,128)(2,1)S(1)} %lightning.1) | data formatting | bytes 1048576

commit v5 on v4

--- a/solution.py
+++ b/solution.py
@@ -36,6 +36,7 @@
     up_out,
     up_in,
     far_in,
+    first_in,
     pz_out,
     pz_in,
     px_out,
@@ -47,9 +48,11 @@
     gain_sem,
     up_ok,
     far_ok,
+    wrap_ok,
     s_sem,
     t_sem,
     up_sem,
+    first_sem,
     pz_sem,
     px_sem,
     sq_sem,
@@ -82,6 +85,9 @@
     odd = lax.rem(high, 2) == 1
     has_down, has_up = high > 0, high < groups - 1
     takes_far = jnp.logical_and(odd, high >= half + 1)
+    chained = jnp.logical_and(high > 0, has_up)
+    relays = jnp.logical_and(high > 0, high < half)
+    beyond = list(range(groups - 1, half, -1))
     sends_far = jnp.logical_and(odd, jnp.logical_and(high >= half - 1, high < groups - 2))
     sends_total = jnp.logical_and(jnp.logical_not(odd), high >= half)
 
@@ -100,6 +106,13 @@
     @pl.when(has_up)
     def _():
         pl.semaphore_signal(barrier, inc=1, device_id={"ctx": z_off(GROUP)}, device_id_type=MESH)
+
+    @pl.when(high == 0)
+    def _():
+        for g in beyond:
+            pl.semaphore_signal(
+                barrier, inc=1, device_id={"ctx": z_off(GROUP * g)}, device_id_type=MESH
+            )
 
     for k in range(1, GROUP):
         pl.semaphore_signal(barrier, inc=1, device_id={"ctx": z_at(k)}, device_id_type=MESH)
@@ -164,6 +177,12 @@
             device_id={"ctx": z_off(2 * GROUP)}, device_id_type=MESH,
         )
 
+    def send_first(source, g, n):
+        return pltpu.make_async_remote_copy(
+            source, first_in, first_sem.at[1 + n], first_sem.at[0],
+            device_id={"ctx": z_off(GROUP * g)}, device_id_type=MESH,
+        )
+
     def send_pz(k):
         return pltpu.make_async_remote_copy(
             pz_out.at[k], pz_in.at[k - 1], pz_sem.at[0, k - 1], pz_sem.at[1, k - 1],
@@ -188,16 +207,28 @@
         def _():
             pl.semaphore_wait(barrier, partners)
 
-        @pl.when(jnp.logical_and(has_down, jnp.logical_not(takes_far)))
+        @pl.when(jnp.logical_and(has_down, high <= half))
         def _():
             pl.semaphore_wait(barrier, partners + 1)
 
+        @pl.when(jnp.logical_and(high > half, jnp.logical_not(odd)))
+        def _():
+            pl.semaphore_wait(barrier, partners + 2)
+
         @pl.when(takes_far)
         def _():
-            pl.semaphore_wait(barrier, partners + 2)
+            pl.semaphore_wait(barrier, partners + 3)
             pl.semaphore_signal(
                 far_ok, inc=1, device_id={"ctx": z_off(-2 * GROUP)}, device_id_type=MESH
             )
+
+        for n, g in enumerate(beyond):
+
+            @pl.when(high == g)
+            def _():
+                pl.semaphore_signal(
+                    wrap_ok.at[n], inc=1, device_id={"ctx": low}, device_id_type=MESH
+                )
 
         @pl.when(has_down)
         def _():
@@ -292,6 +323,7 @@
             else:
                 before[0, index] = value
     group_decay = fixed_decay(rate, z_span * GROUP)
+    first_decay = decay(rate, z_span * GROUP * (high - 1))
 
     @pl.when(has_up)
     def _():
@@ -308,9 +340,15 @@
 
     @pl.when(jnp.logical_not(has_down))
     def _():
+        up_out[...] = whole
+        send_first(up_out, 1, 0).start()
+        first_in[...] = jnp.zeros_like(first_in)
+
+    @pl.when(high <= 1)
+    def _():
         up_in[...] = jnp.zeros_like(up_in)
 
-    @pl.when(has_down)
+    @pl.when(high > 1)
     def _():
         send_up().wait_recv()
 
@@ -319,7 +357,7 @@
         send_far().wait_recv()
         up_in[...] = up_in[...] + group_decay * far_in[...]
 
-    @pl.when(jnp.logical_and(has_up, jnp.logical_not(sends_total)))
+    @pl.when(jnp.logical_and(chained, jnp.logical_not(sends_total)))
     def _():
         up_out[...] = whole + group_decay * up_in[...]
 
@@ -329,7 +367,15 @@
 
         send_up().start()
 
-    incoming = up_in[...]
+    @pl.when(has_down)
+    def _():
+        send_first(first_in, 1, 0).wait_recv()
+
+    @pl.when(relays)
+    def _():
+        send_first(first_in, 1, 0).start()
+
+    incoming = up_in[...] + first_decay * first_in[...]
 
     for k in (3, 2, 1, 0):
         pz_out[k] = pz_out[k] + z_entry[k] * incoming
@@ -405,7 +451,20 @@
         send_t(k).wait_send()
         send_pz(k).wait_send()
 
-    @pl.when(has_up)
+    @pl.when(jnp.logical_not(has_down))
+    def _():
+        for n, g in enumerate(beyond):
+            pl.semaphore_wait(wrap_ok.at[n], 1)
+            send_first(up_out, g, 1 + n).start()
+        send_first(up_out, 1, 0).wait_send()
+        for n, g in enumerate(beyond):
+            send_first(up_out, g, 1 + n).wait_send()
+
+    @pl.when(relays)
+    def _():
+        send_first(first_in, 1, 0).wait_send()
+
+    @pl.when(chained)
     def _():
         send_up().wait_send()
 
@@ -420,6 +479,8 @@
 def solution(mesh):
     nz, nx, nt = mesh.shape["ctx"], mesh.shape["exp"], mesh.shape["tp"]
     slab = HEAD_DIM // GROUP
+    groups = nz // GROUP
+    beyond = groups - 1 - groups // 2
 
     def local(queries, key_vectors, value_vectors, decay_rate, norm_gain):
         rows, width = queries.shape
@@ -444,6 +505,7 @@
             pltpu.VMEM(piece, f32),
             pltpu.VMEM(piece, f32),
             pltpu.VMEM(piece, f32),
+            pltpu.VMEM(piece, f32),
             pltpu.VMEM((GROUP,) + piece, f32),
             pltpu.VMEM((GROUP - 1,) + piece, f32),
             pltpu.VMEM((nx - 1, GROUP) + piece, f32),
@@ -455,9 +517,11 @@
             dma,
             pltpu.SemaphoreType.REGULAR,
             pltpu.SemaphoreType.REGULAR,
+            pltpu.SemaphoreType.REGULAR((beyond,)),
             dma((2, nx - 1, GROUP)),
             dma((2, GROUP - 1)),
             dma((4,)),
+            dma((2 + beyond,)),
             dma((2, GROUP - 1)),
             dma((2, nx - 1, GROUP)),
             dma((2, nt - 1)),

time: 50.8 us -> 46 us (0.906)
  the two profiles are of different devices: /device:TPU:897 before, /device:TPU:673 now
where the time goes in v5:
time: 46 us; the launch traced here: 45.8 us
  Pallas kernels  45 us (98%)
  local copies, waits for them, and re-layouts  0.8 us (2%)
    pallas_call x1, Pallas kernels, local(): pl.pallas_call(functools.partial(kernel, (nz, nx, nt)), out_shape=pltpu.V...  45 us

profile of v5, /device:TPU:673, one launch (start us, length us, event | category | flops | bytes accessed | tf_op | source)
XLA Modules:
  0.0 45.8 jit_solution(10637724611487857261)
XLA Ops:
  0.0 45.0 %lightning.1 = bf16[512,512]{1,0:T(8,128)(2,1)S(1)} custom-call(bf16[512,512]{1,0:T(8,128)(2,1)} %q_hbm.1, bf16[512,512]{1,0:T(8,128)(2,1)} %k_hbm.1, bf16[512,512]{1,0:T(8,128)(2,1)} %v_hbm.1, f32[4]{0:T(128)} %rate_hbm.1, f32[4,128]{1,0:T(4,128)} %bitcast.1), custom_call_target="tpu_custom_call" | custom-call | tf_op jit(solution)/shard_map/lightning/pallas_call | solution.py:529
  45.0 0.8 %copy.7 = bf16[512,512]{1,0:T(8,128)(2,1)} copy(bf16[512,512]{1,0:T(8,128)(2,1)S(1)} %lightning.1) | data formatting | bytes 1048576

commit v6 on v5

--- a/solution.py
+++ b/solution.py
@@ -86,8 +86,8 @@
     has_down, has_up = high > 0, high < groups - 1
     takes_far = jnp.logical_and(odd, high >= half + 1)
     chained = jnp.logical_and(high > 0, has_up)
-    relays = jnp.logical_and(high > 0, high < half)
-    beyond = list(range(groups - 1, half, -1))
+    relays = jnp.logical_and(high > 0, high <= half)
+    beyond = list(range(groups - 1, half + 1, -1))
     sends_far = jnp.logical_and(odd, jnp.logical_and(high >= half - 1, high < groups - 2))
     sends_total = jnp.logical_and(jnp.logical_not(odd), high >= half)
 
@@ -203,21 +203,15 @@
         )
 
     def enter():
-        @pl.when(jnp.logical_not(has_down))
-        def _():
-            pl.semaphore_wait(barrier, partners)
-
-        @pl.when(jnp.logical_and(has_down, high <= half))
-        def _():
-            pl.semaphore_wait(barrier, partners + 1)
-
-        @pl.when(jnp.logical_and(high > half, jnp.logical_not(odd)))
-        def _():
-            pl.semaphore_wait(barrier, partners + 2)
+        below = has_down.astype(jnp.int32) + takes_far + (high > half + 1)
+        for n in range(4):
+
+            @pl.when(below == n)
+            def _():
+                pl.semaphore_wait(barrier, partners + n)
 
         @pl.when(takes_far)
         def _():
-            pl.semaphore_wait(barrier, partners + 3)
             pl.semaphore_signal(
                 far_ok, inc=1, device_id={"ctx": z_off(-2 * GROUP)}, device_id_type=MESH
             )
@@ -237,7 +231,6 @@
             )
 
     position = lax.broadcasted_iota(jnp.int32, (BLK, HEAD_DIM), 0).astype(f32)
-    entered = False
     rate_copy.wait()
     for slot in order:
         rate = rate_of(slot)
@@ -256,12 +249,11 @@
                 first_term[slot, block] = term
             state = term if state is None else block_decay * state + term
         s_own[slot] = state.reshape(GROUP, slab, HEAD_DIM)
-        if not entered:
-            enter()
-            entered = True
-        if slot != 0:
-            for o in (3, 2, 1, 0):
-                send_s(slot, o).start()
+
+    enter()
+    for o in (3, 2, 1, 0):
+        for slot in order[:-1]:
+            send_s(slot, o).start()
 
     line = lax.broadcasted_iota(jnp.int32, (BLK, BLK), 0)
     column = lax.broadcasted_iota(jnp.int32, (BLK, BLK), 1)
@@ -291,23 +283,6 @@
         t_own[o] = plane
         if o:
             send_t(o).start()
-    whole = z_weight[0] * t_own[0]
-    for k in range(1, GROUP):
-        send_t(k).wait_recv()
-        whole = whole + z_weight[k] * t_in[k - 1]
-
-    slabs = [t_own[0]] + [t_in[k - 1] for k in range(1, GROUP)]
-    z_entry = []
-    for k in range(GROUP):
-        goal = low_at(k)
-        z_entry.append(decay(rate, z_span * goal))
-        value = None
-        for j in range(GROUP):
-            if (j + k) % GROUP:
-                source = low_at(-j)
-                term = decay(rate, z_span * (goal - 1 - source), source < goal) * slabs[j]
-                value = term if value is None else value + term
-        pz_out[k] = value
     x_entry = []
     for q in range(nx):
         goal = x_at(q)
@@ -324,6 +299,10 @@
                 before[0, index] = value
     group_decay = fixed_decay(rate, z_span * GROUP)
     first_decay = decay(rate, z_span * GROUP * (high - 1))
+    whole = z_weight[0] * t_own[0]
+    for k in range(1, GROUP):
+        send_t(k).wait_recv()
+        whole = whole + z_weight[k] * t_in[k - 1]
 
     @pl.when(has_up)
     def _():
@@ -343,6 +322,19 @@
         up_out[...] = whole
         send_first(up_out, 1, 0).start()
         first_in[...] = jnp.zeros_like(first_in)
+
+    slabs = [t_own[0]] + [t_in[k - 1] for k in range(1, GROUP)]
+    z_entry = []
+    for k in range(GROUP):
+        goal = low_at(k)
+        z_entry.append(decay(rate, z_span * goal))
+        value = None
+        for j in range(GROUP):
+            if (j + k) % GROUP:
+                source = low_at(-j)
+                term = decay(rate, z_span * (goal - 1 - source), source < goal) * slabs[j]
+                value = term if value is None else value + term
+        pz_out[k] = value
 
     @pl.when(high <= 1)
     def _():
@@ -480,7 +472,7 @@
     nz, nx, nt = mesh.shape["ctx"], mesh.shape["exp"], mesh.shape["tp"]
     slab = HEAD_DIM // GROUP
     groups = nz // GROUP
-    beyond = groups - 1 - groups // 2
+    beyond = max(groups - 2 - groups // 2, 1)
 
     def local(queries, key_vectors, value_vectors, decay_rate, norm_gain):
         rows, width = queries.shape

time: 46 us -> 46.2 us (level)
  the two profiles are of different devices: /device:TPU:673 before, /device:TPU:905 now
where the time goes in v6:
time: 46.2 us; the launch traced here: 46 us
  Pallas kernels  45.2 us (98%)
  local copies, waits for them, and re-layouts  0.8 us (2%)
    pallas_call x1, Pallas kernels, local(): pl.pallas_call(functools.partial(kernel, (nz, nx, nt)), out_shape=pltpu.V...  45.2 us

profile of v6, /device:TPU:905, one launch (start us, length us, event | category | flops | bytes accessed | tf_op | source)
XLA Modules:
  0.0 46.0 jit_solution(15422961598148958278)
XLA Ops:
  0.0 45.2 %lightning.1 = bf16[512,512]{1,0:T(8,128)(2,1)S(1)} custom-call(bf16[512,512]{1,0:T(8,128)(2,1)} %q_hbm.1, bf16[512,512]{1,0:T(8,128)(2,1)} %k_hbm.1, bf16[512,512]{1,0:T(8,128)(2,1)} %v_hbm.1, f32[4]{0:T(128)} %rate_hbm.1, f32[4,128]{1,0:T(4,128)} %bitcast.1), custom_call_target="tpu_custom_call" | custom-call | tf_op jit(solution)/shard_map/lightning/pallas_call | solution.py:521
  45.2 0.8 %copy.7 = bf16[512,512]{1,0:T(8,128)(2,1)} copy(bf16[512,512]{1,0:T(8,128)(2,1)S(1)} %lightning.1) | data formatting | bytes 1048576

commit v7 on v6

--- a/solution.py
+++ b/solution.py
@@ -49,6 +49,7 @@
     up_ok,
     far_ok,
     wrap_ok,
+    first_ok,
     s_sem,
     t_sem,
     up_sem,
@@ -87,6 +88,8 @@
     takes_far = jnp.logical_and(odd, high >= half + 1)
     chained = jnp.logical_and(high > 0, has_up)
     relays = jnp.logical_and(high > 0, high <= half)
+    first_tail = jnp.logical_and(high == 0, low == GROUP - 1)
+    second_head = jnp.logical_and(high == 1, low == 0)
     beyond = list(range(groups - 1, half + 1, -1))
     sends_far = jnp.logical_and(odd, jnp.logical_and(high >= half - 1, high < groups - 2))
     sends_total = jnp.logical_and(jnp.logical_not(odd), high >= half)
@@ -103,9 +106,13 @@
             barrier, inc=1, device_id={"ctx": z_off(2 * GROUP)}, device_id_type=MESH
         )
 
-    @pl.when(has_up)
+    @pl.when(chained)
     def _():
         pl.semaphore_signal(barrier, inc=1, device_id={"ctx": z_off(GROUP)}, device_id_type=MESH)
+
+    @pl.when(second_head)
+    def _():
+        pl.semaphore_signal(barrier, inc=1, device_id={"ctx": z_off(-1)}, device_id_type=MESH)
 
     @pl.when(high == 0)
     def _():
@@ -203,7 +210,7 @@
         )
 
     def enter():
-        below = has_down.astype(jnp.int32) + takes_far + (high > half + 1)
+        below = (high > 1).astype(jnp.int32) + takes_far + (high > half + 1) + first_tail
         for n in range(4):
 
             @pl.when(below == n)
@@ -224,10 +231,16 @@
                     wrap_ok.at[n], inc=1, device_id={"ctx": low}, device_id_type=MESH
                 )
 
-        @pl.when(has_down)
+        @pl.when(high > 1)
         def _():
             pl.semaphore_signal(
                 up_ok, inc=1, device_id={"ctx": z_off(-GROUP)}, device_id_type=MESH
+            )
+
+        @pl.when(first_tail)
+        def _():
+            pl.semaphore_signal(
+                first_ok, inc=1, device_id={"ctx": z_off(1)}, device_id_type=MESH
             )
 
     position = lax.broadcasted_iota(jnp.int32, (BLK, HEAD_DIM), 0).astype(f32)
@@ -283,6 +296,13 @@
         t_own[o] = plane
         if o:
             send_t(o).start()
+
+    @pl.when(second_head)
+    def _():
+        pl.semaphore_wait(first_ok, 1)
+        for k in range(1, GROUP + 1):
+            pl.semaphore_signal(up_ok, inc=1, device_id={"ctx": z_off(-k)}, device_id_type=MESH)
+
     x_entry = []
     for q in range(nx):
         goal = x_at(q)
@@ -510,6 +530,7 @@
             pltpu.SemaphoreType.REGULAR,
             pltpu.SemaphoreType.REGULAR,
             pltpu.SemaphoreType.REGULAR((beyond,)),
+            pltpu.SemaphoreType.REGULAR,
             dma((2, nx - 1, GROUP)),
             dma((2, GROUP - 1)),
             dma((4,)),

time: 46.2 us -> 44.3 us (0.959)
  the two profiles are of different devices: /device:TPU:905 before, /device:TPU:641 now
where the time goes in v7:
time: 44.3 us; the launch traced here: 44.1 us
  Pallas kernels  43.3 us (98%)
  local copies, waits for them, and re-layouts  0.8 us (2%)
    pallas_call x1, Pallas kernels, local(): pl.pallas_call(functools.partial(kernel, (nz, nx, nt)), out_shape=pltpu.V...  43.3 us

profile of v7, /device:TPU:641, one launch (start us, length us, event | category | flops | bytes accessed | tf_op | source)
XLA Modules:
  0.0 44.1 jit_solution(1628807206560509886)
XLA Ops:
  0.0 43.3 %lightning.1 = bf16[512,512]{1,0:T(8,128)(2,1)S(1)} custom-call(bf16[512,512]{1,0:T(8,128)(2,1)} %q_hbm.1, bf16[512,512]{1,0:T(8,128)(2,1)} %k_hbm.1, bf16[512,512]{1,0:T(8,128)(2,1)} %v_hbm.1, f32[4]{0:T(128)} %rate_hbm.1, f32[4,128]{1,0:T(4,128)} %bitcast.1), custom_call_target="tpu_custom_call" | custom-call | tf_op jit(solution)/shard_map/lightning/pallas_call | solution.py:542
  43.3 0.8 %copy.7 = bf16[512,512]{1,0:T(8,128)(2,1)} copy(bf16[512,512]{1,0:T(8,128)(2,1)S(1)} %lightning.1) | data formatting | bytes 1048576

commit v8 on v7

--- a/solution.py
+++ b/solution.py
@@ -87,7 +87,10 @@
     has_down, has_up = high > 0, high < groups - 1
     takes_far = jnp.logical_and(odd, high >= half + 1)
     chained = jnp.logical_and(high > 0, has_up)
-    relays = jnp.logical_and(high > 0, high <= half)
+    relays = jnp.logical_and(odd, high <= half)
+    relays_far = jnp.logical_and(odd, high <= half - 1)
+    hears_far = jnp.logical_and(odd, high >= 3)
+    heard_far = jnp.logical_and(odd, high < groups - 2)
     first_tail = jnp.logical_and(high == 0, low == GROUP - 1)
     second_head = jnp.logical_and(high == 1, low == 0)
     beyond = list(range(groups - 1, half + 1, -1))
@@ -100,7 +103,7 @@
     barrier = pltpu.get_barrier_semaphore()
     partners = (GROUP - 1) + (nx - 1) + (nt - 1)
 
-    @pl.when(sends_far)
+    @pl.when(heard_far)
     def _():
         pl.semaphore_signal(
             barrier, inc=1, device_id={"ctx": z_off(2 * GROUP)}, device_id_type=MESH
@@ -210,14 +213,14 @@
         )
 
     def enter():
-        below = (high > 1).astype(jnp.int32) + takes_far + (high > half + 1) + first_tail
+        below = (high > 1).astype(jnp.int32) + hears_far + (high > half + 1) + first_tail
         for n in range(4):
 
             @pl.when(below == n)
             def _():
                 pl.semaphore_wait(barrier, partners + n)
 
-        @pl.when(takes_far)
+        @pl.when(hears_far)
         def _():
             pl.semaphore_signal(
                 far_ok, inc=1, device_id={"ctx": z_off(-2 * GROUP)}, device_id_type=MESH
@@ -382,6 +385,14 @@
     @pl.when(has_down)
     def _():
         send_first(first_in, 1, 0).wait_recv()
+
+    @pl.when(jnp.logical_and(relays_far, jnp.logical_not(sends_far)))
+    def _():
+        pl.semaphore_wait(far_ok, 1)
+
+    @pl.when(relays_far)
+    def _():
+        send_first(first_in, 2, 1 + len(beyond)).start()
 
     @pl.when(relays)
     def _():
@@ -475,6 +486,10 @@
     @pl.when(relays)
     def _():
         send_first(first_in, 1, 0).wait_send()
+
+    @pl.when(relays_far)
+    def _():
+        send_first(first_in, 2, 1 + len(beyond)).wait_send()
 
     @pl.when(chained)
     def _():
@@ -534,7 +549,7 @@
             dma((2, nx - 1, GROUP)),
             dma((2, GROUP - 1)),
             dma((4,)),
-            dma((2 + beyond,)),
+            dma((3 + beyond,)),
             dma((2, GROUP - 1)),
             dma((2, nx - 1, GROUP)),
             dma((2, nt - 1)),

time: 44.3 us -> 43.7 us (0.986)
  the two profiles are of different devices: /device:TPU:641 before, /device:TPU:929 now
where the time goes in v8:
time: 43.7 us; the launch traced here: 43.6 us
  Pallas kernels  42.8 us (98%)
  local copies, waits for them, and re-layouts  0.8 us (2%)
    pallas_call x1, Pallas kernels, local(): pl.pallas_call(functools.partial(kernel, (nz, nx, nt)), out_shape=pltpu.V...  42.8 us

profile of v8, /device:TPU:929, one launch (start us, length us, event | category | flops | bytes accessed | tf_op | source)
XLA Modules:
  0.0 43.6 jit_solution(2939542344014904256)
XLA Ops:
  0.0 42.8 %lightning.1 = bf16[512,512]{1,0:T(8,128)(2,1)S(1)} custom-call(bf16[512,512]{1,0:T(8,128)(2,1)} %q_hbm.1, bf16[512,512]{1,0:T(8,128)(2,1)} %k_hbm.1, bf16[512,512]{1,0:T(8,128)(2,1)} %v_hbm.1, f32[4]{0:T(128)} %rate_hbm.1, f32[4,128]{1,0:T(4,128)} %bitcast.1), custom_call_target="tpu_custom_call" | custom-call | tf_op jit(solution)/shard_map/lightning/pallas_call | solution.py:557
  42.8 0.8 %copy.7 = bf16[512,512]{1,0:T(8,128)(2,1)} copy(bf16[512,512]{1,0:T(8,128)(2,1)S(1)} %lightning.1) | data formatting | bytes 1048576

commit v9 on v8

--- a/solution.py
+++ b/solution.py
@@ -267,7 +267,9 @@
         s_own[slot] = state.reshape(GROUP, slab, HEAD_DIM)
 
     enter()
-    for o in (3, 2, 1, 0):
+    last_low = low == GROUP - 1
+    slab_order = [jnp.where(last_low, 1, 3), 2, jnp.where(last_low, 3, 1), 0]
+    for o in slab_order:
         for slot in order[:-1]:
             send_s(slot, o).start()
 
@@ -291,13 +293,13 @@
     x_weight = [decay(rate, span * (nx - 1 - x_at(-k))) for k in range(nx)]
     z_span = span * nx
     z_weight = [decay(rate, z_span * (GROUP - 1 - low_at(-k))) for k in range(GROUP)]
-    for o in (3, 2, 1, 0):
+    for n, o in enumerate(slab_order):
         plane = x_weight[0] * s_own[0, low_at(o)]
         for k in range(1, nx):
             send_s(k, o).wait_recv()
             plane = plane + x_weight[k] * s_in[k - 1, low_at(o)]
         t_own[o] = plane
-        if o:
+        if n < GROUP - 1:
             send_t(o).start()
 
     @pl.when(second_head)

time: 43.7 us -> 43.6 us (level)
  the two profiles are of different devices: /device:TPU:929 before, /device:TPU:897 now
where the time goes in v9:
time: 43.6 us; the launch traced here: 43.4 us
  Pallas kernels  42.6 us (98%)
  local copies, waits for them, and re-layouts  0.8 us (2%)
    pallas_call x1, Pallas kernels, local(): pl.pallas_call(functools.partial(kernel, (nz, nx, nt)), out_shape=pltpu.V...  42.6 us

profile of v9, /device:TPU:897, one launch (start us, length us, event | category | flops | bytes accessed | tf_op | source)
XLA Modules:
  0.0 43.4 jit_solution(16280275598348325206)
XLA Ops:
  0.0 42.6 %lightning.1 = bf16[512,512]{1,0:T(8,128)(2,1)S(1)} custom-call(bf16[512,512]{1,0:T(8,128)(2,1)} %q_hbm.1, bf16[512,512]{1,0:T(8,128)(2,1)} %k_hbm.1, bf16[512,512]{1,0:T(8,128)(2,1)} %v_hbm.1, f32[4]{0:T(128)} %rate_hbm.1, f32[4,128]{1,0:T(4,128)} %bitcast.1), custom_call_target="tpu_custom_call" | custom-call | tf_op jit(solution)/shard_map/lightning/pallas_call | solution.py:559
  42.6 0.8 %copy.7 = bf16[512,512]{1,0:T(8,128)(2,1)} copy(bf16[512,512]{1,0:T(8,128)(2,1)S(1)} %lightning.1) | data formatting | bytes 1048576

commit v10 on v8

--- a/solution.py
+++ b/solution.py
@@ -446,16 +446,26 @@
 
     pieces = rows // HEAD_DIM
     per_block = BLK // HEAD_DIM
-    for c in range(pieces):
-        part = squares[c // per_block][(c % per_block) * HEAD_DIM : (c % per_block + 1) * HEAD_DIM]
-        sq_own[pl.ds(c, 1), :] = jnp.sum(part.T, axis=0, keepdims=True)
+    ones = jnp.ones((8, HEAD_DIM), bf16)
+    across = (((1,), (1,)), ((), ()))
+    for block in range(blocks):
+        high_part = squares[block].astype(bf16)
+        low_part = (squares[block] - high_part.astype(f32)).astype(bf16)
+        sums = lax.dot_general(ones, high_part, across, preferred_element_type=f32)
+        sums = sums + lax.dot_general(ones, low_part, across, preferred_element_type=f32)
+        for c in range(per_block):
+            sq_own[pl.ds(block * per_block + c, 1), :] = sums[
+                :1, c * HEAD_DIM : (c + 1) * HEAD_DIM
+            ]
     for k in range(1, nt):
         send_sq(k).start()
+    gain_copy.wait()
+    for slot in range(nx):
+        att[slot] = att[slot] * gain_ref[pl.ds(x_at(slot), 1), :]
     sum_squares = sq_own[...]
     for k in range(1, nt):
         send_sq(k).wait_recv()
         sum_squares = sum_squares + sq_in[k - 1]
-    gain_copy.wait()
     scale = lax.rsqrt(sum_squares / (nt * nx * HEAD_DIM) + 1e-06)
     for c in range(pieces):
         at = pl.ds(c * HEAD_DIM, HEAD_DIM)
@@ -463,8 +473,7 @@
         for slot in range(nx):
             head = x_at(slot)
             lanes = pl.ds(pl.multiple_of(head * HEAD_DIM, HEAD_DIM), HEAD_DIM)
-            gain = gain_ref[pl.ds(head, 1), :]
-            out_ref[at, lanes] = (att[slot, at, :] * row_scale * gain).astype(bf16)
+            out_ref[at, lanes] = (att[slot, at, :] * row_scale).astype(bf16)
 
     for k in range(1, nx):
         for c in range(GROUP):

time: 43.7 us -> 43.9 us (level)
  no operation moved by 1% of the time
where the time goes in v10:
time: 43.9 us; the launch traced here: 43.7 us
  Pallas kernels  42.9 us (98%)
  local copies, waits for them, and re-layouts  0.8 us (2%)
    pallas_call x1, Pallas kernels, local(): pl.pallas_call(functools.partial(kernel, (nz, nx, nt)), out_shape=pltpu.V...  42.9 us

profile of v10, /device:TPU:929, one launch (start us, length us, event | category | flops | bytes accessed | tf_op | source)
XLA Modules:
  0.0 43.7 jit_solution(991104389846875676)
XLA Ops:
  0.0 42.9 %lightning.1 = bf16[512,512]{1,0:T(8,128)(2,1)S(1)} custom-call(bf16[512,512]{1,0:T(8,128)(2,1)} %q_hbm.1, bf16[512,512]{1,0:T(8,128)(2,1)} %k_hbm.1, bf16[512,512]{1,0:T(8,128)(2,1)} %v_hbm.1, f32[4]{0:T(128)} %rate_hbm.1, f32[4,128]{1,0:T(4,128)} %bitcast.1), custom_call_target="tpu_custom_call" | custom-call | tf_op jit(solution)/shard_map/lightning/pallas_call | solution.py:566
  42.9 0.8 %copy.7 = bf16[512,512]{1,0:T(8,128)(2,1)} copy(bf16[512,512]{1,0:T(8,128)(2,1)S(1)} %lightning.1) | data formatting | bytes 1048576
